TPU v7x, 32 devices: a whole 2x2x4 slice. The times are simulated.
32 devices in a mesh: groups: 2 (over x), seq: 16 (over z, y, core).
Axes of the slice: x: 2, y: 2, z: 4, core: 2. Of those that a mesh axis runs over, the one named last changes fastest.
Arguments:
- hidden: bfloat16 [16384, 320], P(('groups', 'seq')), parts along dimension 0, may hold values from -20 to 20
- ref_hidden: bfloat16 [2048, 320], P(('groups', 'seq')), parts along dimension 0, may hold values from -6 to 6
- visible: int32 [128, 64], P('groups'), parts along dimension 0, may hold values 0 or 1
- ref_count: int32 [2], P('groups'), parts along dimension 0, may hold values from 256 to 1024
- w_query: bfloat16 [320, 320], replicated, may hold values from -0.3125 to 0.3125
- w_key: bfloat16 [320, 320], replicated, may hold values from -0.3125 to 0.3125
- w_value: bfloat16 [320, 320], replicated, may hold values from -0.3125 to 0.3125
- w_out: bfloat16 [320, 320], replicated, may hold values from -0.3125 to 0.3125
Outputs:
- attended: bfloat16 [16384, 320], P(('groups', 'seq')), parts along dimension 0
There are 2 independent parts, one for each index of `groups`. A program takes and returns all parts, laid end to end along the dimension named above; an argument that names none is the same for every part. Nothing has to cross between parts.
All inputs are finite; a program needn't handle non-finite values.
Results may differ from a plain program's by a relative error of at most 0.011.
Values may be sent and summed in bfloat16 or wider, within the bound.
A program may use at most 128 MiB of HBM per device.

v0:
```python
import math

import jax
import jax.numpy as jnp
from jax import lax
from jax.sharding import PartitionSpec as P

HEADS = 5
TILE = 128
TILES_VIEW = 8


def project(states, weight, head_count):
    result = jnp.dot(states, weight, preferred_element_type=jnp.float32).astype(jnp.bfloat16)
    return result.reshape(states.shape[0], head_count, weight.shape[1] // head_count)


def local(hidden, ref_hidden, visible, ref_count, w_query, w_key, w_value, w_out):
    row_count = hidden.shape[0]
    width = hidden.shape[1]
    head_count = HEADS
    head_size = width // head_count
    scale = 1.0 / math.sqrt(head_size)
    tile_count = visible.shape[0]
    view_tiles = TILES_VIEW
    row_start = lax.axis_index("seq") * row_count
    queries = project(hidden, w_query, head_count)
    row_tile = (row_start + jnp.arange(row_count, dtype=jnp.int32)) // TILE
    row_view = row_tile // view_tiles
    picker = (row_tile[:, None] == jnp.arange(tile_count, dtype=jnp.int32)[None, :]).astype(
        jnp.float32
    )
    seen_tiles = jnp.dot(picker, visible.astype(jnp.float32))

    def attend(state, key_rows, value_rows, allowed):
        run_max, run_total, run_acc = state
        scores = (
            jnp.einsum("qhd,khd->hqk", queries, key_rows, preferred_element_type=jnp.float32)
            * scale
        )
        scores = jnp.where(allowed[None, :, :], scores, jnp.float32(-1e30))
        new_max = jnp.maximum(run_max, jnp.max(scores, axis=-1))
        expo = jnp.exp(scores - new_max[:, :, None])
        factor = jnp.exp(run_max - new_max)
        new_total = run_total * factor + jnp.sum(expo, axis=-1)
        new_acc = run_acc * factor[:, :, None] + jnp.einsum(
            "hqk,khd->hqd",
            expo.astype(jnp.bfloat16),
            value_rows,
            preferred_element_type=jnp.float32,
        )
        return (new_max, new_total, new_acc)

    def view_block(state, key_rows, value_rows, offset):
        key_count = key_rows.shape[0]
        key_tile = (offset + jnp.arange(key_count, dtype=jnp.int32)) // TILE
        onehot = (key_tile[:, None] == jnp.arange(tile_count, dtype=jnp.int32)[None, :]).astype(
            jnp.float32
        )
        tile_hits = jnp.dot(seen_tiles, onehot.T)
        allowed = (tile_hits > 0.5) | (row_view[:, None] == (key_tile // view_tiles)[None, :])
        return attend(state, key_rows, value_rows, allowed)

    local_keys = jnp.dot(ref_hidden, w_key, preferred_element_type=jnp.float32).astype(jnp.bfloat16)
    local_values = jnp.dot(ref_hidden, w_value, preferred_element_type=jnp.float32).astype(
        jnp.bfloat16
    )
    ref_keys, ref_values = (
        lax.all_gather(local_keys, "seq", axis=0, tiled=True),
        lax.all_gather(local_values, "seq", axis=0, tiled=True),
    )
    ref_keys = ref_keys.reshape(ref_keys.shape[0], head_count, head_size)
    ref_values = ref_values.reshape(ref_values.shape[0], head_count, head_size)
    ref_total = ref_keys.shape[0]
    ref_allowed = jnp.broadcast_to(
        (jnp.arange(ref_total, dtype=jnp.int32) < ref_count[0])[None, :], (row_count, ref_total)
    )
    initial = (
        jnp.full((head_count, row_count), -1e30, jnp.float32),
        jnp.zeros((head_count, row_count), jnp.float32),
        jnp.zeros((head_count, row_count, head_size), jnp.float32),
    )
    state = attend(initial, ref_keys, ref_values, ref_allowed)
    view_keys = project(hidden, w_key, head_count)
    view_values = project(hidden, w_value, head_count)
    pieces = (
        lax.all_gather(view_keys, "seq", axis=0, tiled=True),
        lax.all_gather(view_values, "seq", axis=0, tiled=True),
    )
    sweep_state = state
    key_rows = pieces[0]
    value_rows = pieces[1]
    key_count = key_rows.shape[0]
    block_size = 512
    block_count = key_count // block_size
    key_blocks = key_rows.reshape(block_count, block_size, head_count, head_size)
    value_blocks = value_rows.reshape(block_count, block_size, head_count, head_size)

    def advance(inner, pieces):
        block_index, key_part, value_part = pieces
        return (view_block(inner, key_part, value_part, block_index * block_size), None)

    sweep_state, unused = lax.scan(
        advance, sweep_state, (jnp.arange(block_count, dtype=jnp.int32), key_blocks, value_blocks)
    )
    state = sweep_state
    run_max, run_total, run_acc = state
    mixed = run_acc / run_total[:, :, None]
    mixed = jnp.transpose(mixed, (1, 0, 2)).reshape(row_count, width).astype(jnp.bfloat16)
    return jnp.dot(mixed, w_out, preferred_element_type=jnp.float32).astype(jnp.bfloat16)


def solution(mesh):
    in_specs = (
        P(("groups", "seq"), None),
        P(("groups", "seq"), None),
        P("groups", None),
        P("groups"),
        P(),
        P(),
        P(),
        P(),
    )
    out_specs = P(("groups", "seq"), None)
    return jax.shard_map(local, mesh=mesh, in_specs=in_specs, out_specs=out_specs, check_vma=False)
```

profile of v0, /device:TPU:0, one launch (start us, length us, event | category | flops | bytes accessed | tf_op | source)
XLA Modules:
  0.0 273.2 jit_solution(13204093446191117111)
XLA Ops:
  6.5 1.0 copy-done
  7.5 2.0 convolution_convert_fusion.1
  9.6 2.0 convolution_convert_fusion.2
  12.3 1.1 convolution_convert_fusion.5
  13.5 28.4 %all_gather.12 = bf16[1024,320]{1,0:T(8,128)(2,1)S(1)} all-gather(bf16[64,320]{1,0:T(8,128)(2,1)S(1)} %convolution_convert_fusion.5), channel_id=1, replica_groups=mesh['groups'=2,'seq'=16] {'seq'}, dimensions={0}, use_global_device_ids=true | all-gather | bytes 696320 | tf_op jit(solution)/shard_map/all_gather | solution.py:69
  42.1 1.1 convolution_convert_fusion.4
  43.3 24.3 %all_gather.13 = bf16[1024,320]{1,0:T(8,128)(2,1)S(1)} all-gather(bf16[64,320]{1,0:T(8,128)(2,1)S(1)} %convolution_convert_fusion.4), channel_id=1, replica_groups=mesh['groups'=2,'seq'=16] {'seq'}, dimensions={0}, use_global_device_ids=true | all-gather | bytes 696320 | tf_op jit(solution)/shard_map/all_gather | solution.py:70
  68.2 1.7 fusion.33
  69.9 2.5 fusion.35
  72.7 2.3 fusion.39
  75.0 4.0 %all-gather.5.cloned.1.call-done = bf16[8192,5,64]{0,2,1:T(8,128)(2,1)} async-done(((bf16[512,5,64]{0,2,1:T(8,128)(2,1)}), bf16[8192,5,64]{0,2,1:T(8,128)(2,1)}) %all-gather.5.cloned.1.call-update) | async-done | bytes 5242896 | tf_op jit(solution)/shard_map/all_gather | solution.py:88
  79.0 5.6 %copy.25 = bf16[5,8,16,8,512]{4,3,1,0,2:T(8,128)(2,1)} copy(bf16[5,8,16,8,512]{4,3,2,1,0:T(8,128)(2,1)} %bitcast.81) | data formatting | bytes 10485760 | tf_op jit(solution)/shard_map/reshape | solution.py:97
  84.6 56.0 %all-gather.3.cloned.1.call-done = bf16[8192,5,64]{0,2,1:T(8,128)(2,1)} async-done(((bf16[512,5,64]{0,2,1:T(8,128)(2,1)}), bf16[8192,5,64]{0,2,1:T(8,128)(2,1)}) %all-gather.3.cloned.1.call-update) | async-done | bytes 5242896 | tf_op jit(solution)/shard_map/all_gather | solution.py:87
  140.6 5.6 %copy.26 = bf16[5,8,16,8,512]{4,3,1,0,2:T(8,128)(2,1)} copy(bf16[5,8,16,8,512]{4,3,2,1,0:T(8,128)(2,1)} %bitcast.82) | data formatting | bytes 10485760 | tf_op jit(solution)/shard_map/reshape | solution.py:96
  146.2 118.9 %while.18 = (s32[]{:T(128)}, f32[5,512]{1,0:T(8,128)S(1)}, f32[5,512]{1,0:T(8,128)S(1)}, f32[5,512,64]{1,2,0:T(8,128)S(1)}, s32[16]{0:T(128)S(1)}, /*index=5*/bf...) while((s32[]{:T(128)}, f32[5,512]{1,0:T(8,128)S(1)}, ...), condition=%wide.region_5.6_spmd.clone, body=%wide.region_2.5_spmd.clone.sunk | while | flops 384700416 | bytes 19313812 | solution.py:103
  147.9 2.0 fusion.81
  150.0 1.1 fusion.82
  151.1 2.5 fusion.83
  155.3 2.0 fusion.81
  157.4 1.1 fusion.82
  158.5 2.5 fusion.83
  162.8 2.0 fusion.81
  164.8 1.1 fusion.82
  166.0 2.5 fusion.83
  170.2 2.0 fusion.81
  172.3 1.1 fusion.82
  173.4 2.5 fusion.83
  177.6 2.0 fusion.81
  179.7 1.1 fusion.82
  180.8 2.5 fusion.83
  185.1 2.0 fusion.81
  187.1 1.1 fusion.82
  188.3 2.5 fusion.83
  192.5 2.0 fusion.81
  194.6 1.1 fusion.82
  195.7 2.5 fusion.83
  199.9 2.0 fusion.81
  202.0 1.1 fusion.82
  203.1 2.5 fusion.83
  207.4 2.0 fusion.81
  209.4 1.1 fusion.82
  210.6 2.5 fusion.83
  214.8 2.0 fusion.81
  216.9 1.1 fusion.82
  218.0 2.5 fusion.83
  222.2 2.0 fusion.81
  224.3 1.1 fusion.82
  225.4 2.5 fusion.83
  229.7 2.0 fusion.81
  231.7 1.1 fusion.82
  232.9 2.5 fusion.83
  237.1 2.0 fusion.81
  239.2 1.1 fusion.82
  240.3 2.5 fusion.83
  244.5 2.0 fusion.81
  246.6 1.1 fusion.82
  247.7 2.5 fusion.83
  252.0 2.0 fusion.81
  254.0 1.1 fusion.82
  255.2 2.5 fusion.83
  259.4 2.0 fusion.81
  261.5 1.1 fusion.82
  262.6 2.5 fusion.83
  265.2 1.1 convolution_convert_fusion
  (133 shorter events, 17.9 us)
Async XLA Ops:
  6.5 1.0 copy-start
  6.5 61.3 %copy-start.1 = (bf16[320,320]{1,0:T(8,128)(2,1)S(1)}, bf16[320,320]{1,0:T(8,128)(2,1)}, u32[]{:S(2)}) copy-start(bf16[320,320]{1,0:T(8,128)(2,1)} %param.14) | copy-start | bytes 614404
  6.5 72.5 %all-gather.5.cloned.1.call-start = ((), (), s32[]{:S(2)}) async-start(), calls=%async_computation.1 | async-start | bytes 5570560 | tf_op jit(solution)/shard_map/all_gather | solution.py:88
  9.6 131.1 %all-gather.3.cloned.1.call-start = ((), (), s32[]{:S(2)}) async-start(), calls=%async_computation | async-start | bytes 5570560 | tf_op jit(solution)/shard_map/all_gather | solution.py:87
  69.9 2.5 copy-start.3
  146.2 119.0 %copy-start.2 = (bf16[320,320]{1,0:T(8,128)(2,1)S(1)}, bf16[320,320]{1,0:T(8,128)(2,1)}, u32[]{:S(2)}) copy-start(bf16[320,320]{1,0:T(8,128)(2,1)} %param.17) | copy-start | bytes 614404
Sparse Core Ops, SparseCore 0:
  9.7 69.3 all-gather.4
  81.2 59.3 all-gather.2
where the time goes:
time: 275 us; the launch traced here: 273 us
  matrix products  91.4 us (33%)
  waiting for transfers between devices  60.1 us (22%)
  blocking collectives  52.6 us (19%)
  local copies, waits for them, and re-layouts  22.1 us (8%)
  other arithmetic  21.1 us (8%)
  between operations  14.2 us (5%)
  loops' own time  11.7 us (4%)
    all_gather x1, waiting for transfers between devices, local(): lax.all_gather(view_keys, 'seq', axis=0, tiled=True)  56 us
    dot_general x17, matrix products, attend(): jnp.einsum('hqk,khd->hqd', expo.astype(jnp.bfloat16), value_rows, preferr...  42.9 us
    dot_general x17, matrix products, attend(): jnp.einsum('qhd,khd->hqk', queries, key_rows, preferred_element_type=jnp....  34.2 us
    all_gather x1, blocking collectives, local(): lax.all_gather(local_keys, 'seq', axis=0, tiled=True)  28.4 us
    all_gather x1, blocking collectives, local(): lax.all_gather(local_values, 'seq', axis=0, tiled=True)  24.3 us
    reduce_sum x17, other arithmetic, attend(): new_total = run_total * factor + jnp.sum(expo, axis=-1)  20.1 us
    another operation x1, loops' own time, local(): lax.scan(advance, sweep_state, (jnp.arange(block_count, dtype=jnp.int32),...  11.7 us
    dynamic_slice x16, local copies, waits for them, and re-layouts, local(): lax.scan(advance, sweep_state, (jnp.arange(block_count, dtype=jnp.int32),...  9.38 us
  transfers between devices with their start and end apart: 2, of which 2 were waited for; matrix products, arithmetic and copies ran while one was open for 6% of the time, Pallas kernels for 0%

commit v1 on v0

v1 whole, which is shorter than its diff:
```python
import functools
import math

import jax
import jax.numpy as jnp
from jax import lax
from jax.experimental import pallas as pl
from jax.experimental.pallas import tpu as pltpu
from jax.sharding import PartitionSpec as P

HEADS = 5
TILE = 128
TILES_VIEW = 8
NEG = -1e30
F32 = jnp.float32
BF16 = jnp.bfloat16


def lanes(width):
    return -(-width // 128) * 128


def nt(a, b):
    return lax.dot_general(a, b, (((1,), (1,)), ((), ())), preferred_element_type=F32)


def tn(a, b):
    return lax.dot_general(a, b, (((0,), (0,)), ((), ())), preferred_element_type=F32)


def prepare(hidden_ref, visible_ref, wq_ref, wk_ref, wv_ref, wkp, wvt, qz, vis, m_s, acc_s, me):
    rows, width = hidden_ref.shape
    size = width // HEADS
    pad = lanes(width)
    shift = pad - width
    tiles = visible_ref.shape[0]
    wkp[...] = jnp.zeros_like(wkp)
    wkp[0, :width, :width] = wk_ref[...]
    wkp[1, shift:, :width] = wk_ref[...]
    wvt_val = wv_ref[...].T
    wvt[...] = jnp.zeros_like(wvt)
    wvt[0, :, :width] = wvt_val
    wvt[1, :, shift:] = wvt_val
    scale = math.log2(math.e) / math.sqrt(size)
    q = jnp.dot(hidden_ref[...], wq_ref[...], preferred_element_type=F32) * scale
    qt = q.T.astype(BF16)
    qz[...] = jnp.zeros_like(qz)
    for h in range(HEADS):
        base = (h % 2) * size
        qz[h, base:base + size, :] = qt[h * size:(h + 1) * size]
    first = me * (rows // TILE)
    q_tile = first + lax.broadcasted_iota(jnp.int32, (tiles, rows), 1) // TILE
    k_tile = lax.broadcasted_iota(jnp.int32, (tiles, rows), 0)
    pick = (k_tile == q_tile).astype(BF16)
    seen = tn(visible_ref[...].astype(F32).astype(BF16), pick)
    own = (q_tile // TILES_VIEW) == (k_tile // TILES_VIEW)
    vis[...] = jnp.where((seen > 0.5) | own, F32(1.0), F32(0.0))
    m_s[...] = jnp.full_like(m_s, NEG)
    acc_s[...] = jnp.zeros_like(acc_s)


def absorb(x, wkp, wvt, qz, m_s, acc_s, width, vis_rows, limit):
    size = width // HEADS
    pad = lanes(width)
    half = x.shape[0]
    x_lo, x_hi = x[:, :pad], x[:, 2 * width - pad:]
    keys = jnp.concatenate(
        [
            jnp.dot(x_lo, wkp[0], preferred_element_type=F32).astype(BF16),
            jnp.dot(x_hi, wkp[1], preferred_element_type=F32).astype(BF16),
        ],
        axis=0,
    )
    values = [nt(wvt[0], x_lo).astype(BF16), nt(wvt[1], x_hi).astype(BF16)]
    ones = jnp.ones((16, half), BF16)
    for h in range(HEADS):
        s = jnp.dot(
            keys[:, (h // 2) * 128:(h // 2) * 128 + 128], qz[h], preferred_element_type=F32
        )
        m_old = m_s[h:h + 1, :]
        if vis_rows is None:
            part, at_lo, at_hi = limit
            ids = lax.broadcasted_iota(jnp.int32, (half, 1), 0)
            s = jnp.where(jnp.concatenate([at_lo(ids), at_hi(ids)], axis=0) < part, s, NEG)
            m_new = jnp.maximum(m_old, jnp.max(s, axis=0, keepdims=True))
            p = jnp.exp2(s - m_new).astype(BF16)
        else:
            tops = []
            for t, ok in enumerate(vis_rows):
                top = jnp.max(s[t * TILE:(t + 1) * TILE], axis=0, keepdims=True)
                tops.append(jnp.where(ok, top, NEG))
            m_new = functools.reduce(jnp.maximum, tops, m_old)
            parts = []
            for t, ok in enumerate(vis_rows):
                less = jnp.where(ok, m_new, F32(-NEG))
                parts.append(jnp.exp2(s[t * TILE:(t + 1) * TILE] - less).astype(BF16))
            p = jnp.concatenate(parts, axis=0)
        fade = jnp.exp2(m_old - m_new)
        m_s[h:h + 1, :] = m_new
        total = acc_s[h] * fade
        for k in range(2):
            v = jnp.concatenate([values[k][h * size:(h + 1) * size], ones], axis=0)
            total = total + jnp.dot(
                v, p[k * half:(k + 1) * half], preferred_element_type=F32
            )
        acc_s[h] = total


def finish(out_ref, wo_ref, acc_s, width):
    size = width // HEADS
    out = None
    for h in range(HEADS):
        mixed = (acc_s[h, :size] / acc_s[h, size:size + 1]).T.astype(BF16)
        term = jnp.dot(mixed, wo_ref[h * size:(h + 1) * size], preferred_element_type=F32)
        out = term if out is None else out + term
    out_ref[...] = out.astype(BF16)


def kernel(count_ref, gathered_ref, hidden_ref, visible_ref, wq_ref, wk_ref, wv_ref, wo_ref,
           out_ref, wkp, wvt, qz, vis, m_s, acc_s, refs):
    n = gathered_ref.shape[0]
    rows, width = hidden_ref.shape
    half = rows // 2
    ref_half = gathered_ref.shape[1] - half
    me = lax.axis_index("seq")
    prepare(hidden_ref, visible_ref, wq_ref, wk_ref, wv_ref, wkp, wvt, qz, vis, m_s, acc_s, me)
    tiles = rows // TILE

    def step(i, carry):
        j = lax.rem(me + i, n)
        vis_rows = [vis[pl.ds(j * tiles + t, 1), :] > 0.5 for t in range(tiles)]
        absorb(gathered_ref[j, :half], wkp, wvt, qz, m_s, acc_s, width, vis_rows, None)
        return carry

    lax.fori_loop(0, n, step, 0)
    for j in range(n):
        refs[j * ref_half:(j + 1) * ref_half] = gathered_ref[j, half:]
    count = count_ref[0]
    block = half
    for b in range(n * ref_half // block):
        def at(ids, extra, b=b):
            r = ids + b * block
            return (r // ref_half) * (2 * ref_half) + r % ref_half + extra
        absorb(refs[b * block:(b + 1) * block], wkp, wvt, qz, m_s, acc_s, width, None,
               (count, lambda ids: at(ids, 0), lambda ids: at(ids, ref_half)))
    finish(out_ref, wo_ref, acc_s, width)


def pack(x):
    half = x.shape[0] // 2
    return jnp.concatenate([x[:half], x[half:]], axis=1)


def local(hidden, ref_hidden, visible, ref_count, w_query, w_key, w_value, w_out):
    rows, width = hidden.shape
    size = width // HEADS
    pad = lanes(width)
    mine = jnp.concatenate([pack(hidden), pack(ref_hidden)], axis=0)
    gathered = lax.all_gather(mine, "seq", axis=0, tiled=False)
    n = gathered.shape[0]
    vmem = pl.BlockSpec(memory_space=pltpu.VMEM)
    return pl.pallas_call(
        kernel,
        out_shape=jax.ShapeDtypeStruct((rows, width), BF16),
        in_specs=[pl.BlockSpec(memory_space=pltpu.SMEM)] + [vmem] * 7,
        out_specs=vmem,
        scratch_shapes=[
            pltpu.VMEM((2, pad, pad), BF16),
            pltpu.VMEM((2, width, pad), BF16),
            pltpu.VMEM((HEADS, 128, rows), BF16),
            pltpu.VMEM((visible.shape[0], rows), F32),
            pltpu.VMEM((8, rows), F32),
            pltpu.VMEM((HEADS, size + 16, rows), F32),
            pltpu.VMEM((n * ref_hidden.shape[0] // 2, 2 * width), BF16),
        ],
        compiler_params=pltpu.CompilerParams(vmem_limit_bytes=56 << 20),
    )(ref_count, gathered, hidden, visible, w_query, w_key, w_value, w_out)


def solution(mesh):
    in_specs = (
        P(("groups", "seq"), None),
        P(("groups", "seq"), None),
        P("groups", None),
        P("groups"),
        P(),
        P(),
        P(),
        P(),
    )
    out_specs = P(("groups", "seq"), None)
    return jax.shard_map(local, mesh=mesh, in_specs=in_specs, out_specs=out_specs, check_vma=False)
```

time: 275 us -> 138 us (0.50)
  matrix products: 91.4 us -> 0 us
  Pallas kernels: 0 us -> 57.8 us
  blocking collectives: 52.6 us -> 0 us
  other arithmetic: 21.1 us -> 0.87 us
  local copies, waits for them, and re-layouts: 22.1 us -> 3.86 us
  loops' own time: 11.7 us -> 0 us
    dot_general x57 -> x0, matrix products: 91.4 us -> none  [the longest x17 42.9 us: attend(): jnp.einsum('hqk,khd->hqd', expo.astype(jnp.bfloat16), value_rows, preferr...]
    pallas_call x0 -> x1, Pallas kernels: none -> 57.8 us  [local(): pl.pallas_call(kernel, out_shape=jax.ShapeDtypeStruct((rows, width), BF16...]
    all_gather x2 -> x0, blocking collectives: 52.6 us -> none  [the longest x1 28.4 us: local(): lax.all_gather(local_keys, 'seq', axis=0, tiled=True)]
    reduce_sum x17 -> x0, other arithmetic: 20.1 us -> none  [attend(): new_total = run_total * factor + jnp.sum(expo, axis=-1)]
    another operation x1 -> x0, loops' own time: 11.7 us -> none  [local(): lax.scan(advance, sweep_state, (jnp.arange(block_count, dtype=jnp.int32),...]
    reshape x2 -> x0, local copies, waits for them, and re-layouts: 11.2 us -> none  [the longest x1 5.59 us: local(): key_rows.reshape(block_count, block_size, head_count, head_size)]
    dynamic_slice x16 -> x0, local copies, waits for them, and re-layouts: 9.38 us -> none  [local(): lax.scan(advance, sweep_state, (jnp.arange(block_count, dtype=jnp.int32),...]
    all_gather x2 -> x1, waiting for transfers between devices: 60 us -> 61.6 us  [local(): gathered = lax.all_gather(mine, 'seq', axis=0, tiled=False)]
  transfers between devices with their start and end apart: 2 -> 1, of which waited for: 2 -> 1; matrix products, arithmetic and copies ran while one was open for 6% -> 0% of each run, Pallas kernels for 0% -> 0%
where the time goes in v1:
time: 138 us
  waiting for transfers between devices  61.6 us (45%)
  Pallas kernels  57.8 us (42%)
  between operations  14.1 us (10%)
  local copies, waits for them, and re-layouts  3.86 us (3%)
    all_gather x1, waiting for transfers between devices, local(): gathered = lax.all_gather(mine, 'seq', axis=0, tiled=False)  61.6 us
    pallas_call x1, Pallas kernels, local(): pl.pallas_call(kernel, out_shape=jax.ShapeDtypeStruct((rows, width), BF16...  57.8 us
  transfers between devices with their start and end apart: 1, of which 1 were waited for; matrix products, arithmetic and copies ran while one was open for 0% of the time, Pallas kernels for 0%

profile of v1, /device:TPU:0, one launch (start us, length us, event | category | flops | bytes accessed | tf_op | source)
XLA Modules:
  0.0 138.2 jit_solution(17801280403964888290)
XLA Ops:
  6.5 0.0 all-gather.3.cloned.1.call-start
  6.5 0.8 fusion.1
  7.3 1.2 copy.13.hidden_ref
  8.5 0.0 copy-start
  8.5 0.9 maximum_maximum_fusion
  9.4 0.0 all-gather.3.cloned.1.call-update
  10.1 61.6 %all-gather.3.cloned.1.call-done = bf16[4608,640]{1,0:T(8,128)(2,1)} async-done(((bf16[288,640]{1,0:T(8,128)(2,1)}), bf16[4608,640]{1,0:T(8,128)(2,1)}) %all-gather.3.cloned.1.call-update) | async-done | bytes 5898256 | tf_op jit(solution)/shard_map/all_gather | solution.py:159
  71.7 0.0 copy-done
  71.7 57.8 %shard_map.82 = bf16[512,320]{1,0:T(8,128)(2,1)} custom-call(s32[1]{0:T(128)S(6)} %copy.17.count_ref, bf16[16,288,640]{2,1,0:T(8,128)(2,1)} %bitcast.1, bf16[512,320]{1,0:T(8,128)(2,1)} %copy-done, s32[64,64]{1,0:T(8,128)} %visible_ref.1, bf16[320,320]{1,0:T(8,128)(2,1)} %wq_ref.1, bf16[320,320]{1,0:T(8,128)(2,1)} %wk_ref.1, bf16[320,320]{1,0:T(8,128)(2,1)} %wv_ref.1, ...), custom_call_target="tpu_custom_call" | custom-call | tf_op jit(solution)/shard_map/pallas_call | solution.py:162
  129.4 1.9 %copy.16 = bf16[512,320]{0,1:T(8,128)(2,1)} copy(bf16[512,320]{1,0:T(8,128)(2,1)} %shard_map.82) | data formatting | bytes 655360 | tf_op jit(solution)/shard_map/pallas_call | solution.py:162
  (1 shorter events, 0.0 us)
Async XLA Ops:
  6.5 65.1 %all-gather.3.cloned.1.call-start = ((), (), s32[]{:S(2)}) async-start(), calls=%async_computation | async-start | bytes 6266880 | tf_op jit(solution)/shard_map/all_gather | solution.py:159
  8.5 63.2 %copy-start = (bf16[512,320]{1,0:T(8,128)(2,1)}, bf16[512,320]{1,0:T(8,128)(2,1)S(1)}, u32[]{:S(2)}) copy-start(bf16[512,320]{1,0:T(8,128)(2,1)S(1)} %copy.13.hidden_ref) | copy-start | bytes 983044
Sparse Core Ops, SparseCore 0:
  9.6 62.0 all-gather.2

commit v2 on v1

--- a/solution.py
+++ b/solution.py
@@ -28,8 +28,10 @@
     return lax.dot_general(a, b, (((0,), (0,)), ((), ())), preferred_element_type=F32)
 
 
-def prepare(hidden_ref, visible_ref, wq_ref, wk_ref, wv_ref, wkp, wvt, qz, vis, m_s, acc_s, me):
-    rows, width = hidden_ref.shape
+def prepare(mine_ref, visible_ref, wq_ref, wk_ref, wv_ref, wkp, wvt, qz, vis, m_s, acc_s, me):
+    rows = qz.shape[2]
+    half = rows // 2
+    width = mine_ref.shape[1] // 2
     size = width // HEADS
     pad = lanes(width)
     shift = pad - width
@@ -42,7 +44,17 @@
     wvt[0, :, :width] = wvt_val
     wvt[1, :, shift:] = wvt_val
     scale = math.log2(math.e) / math.sqrt(size)
-    q = jnp.dot(hidden_ref[...], wq_ref[...], preferred_element_type=F32) * scale
+    wq = wq_ref[...]
+    gap = jnp.zeros((shift, width), BF16)
+    q = jnp.concatenate(
+        [
+            jnp.dot(mine_ref[:half, :pad], jnp.concatenate([wq, gap], axis=0),
+                    preferred_element_type=F32),
+            jnp.dot(mine_ref[:half, 2 * width - pad:], jnp.concatenate([gap, wq], axis=0),
+                    preferred_element_type=F32),
+        ],
+        axis=0,
+    ) * scale
     qt = q.T.astype(BF16)
     qz[...] = jnp.zeros_like(qz)
     for h in range(HEADS):
@@ -116,34 +128,137 @@
     out_ref[...] = out.astype(BF16)
 
 
-def kernel(count_ref, gathered_ref, hidden_ref, visible_ref, wq_ref, wk_ref, wv_ref, wo_ref,
-           out_ref, wkp, wvt, qz, vis, m_s, acc_s, refs):
-    n = gathered_ref.shape[0]
-    rows, width = hidden_ref.shape
+def kernel(n, count_ref, mine_ref, visible_ref, wq_ref, wk_ref, wv_ref, wo_ref,
+           out_ref, buf, wkp, wvt, qz, vis, m_s, acc_s, refs, send_sem, recv_sem, own_sem):
+    width = mine_ref.shape[1] // 2
+    rows = qz.shape[2]
     half = rows // 2
-    ref_half = gathered_ref.shape[1] - half
+    ref_half = mine_ref.shape[0] - half
+    tiles = rows // TILE
     me = lax.axis_index("seq")
-    prepare(hidden_ref, visible_ref, wq_ref, wk_ref, wv_ref, wkp, wvt, qz, vis, m_s, acc_s, me)
-    tiles = rows // TILE
-
-    def step(i, carry):
-        j = lax.rem(me + i, n)
-        vis_rows = [vis[pl.ds(j * tiles + t, 1), :] > 0.5 for t in range(tiles)]
-        absorb(gathered_ref[j, :half], wkp, wvt, qz, m_s, acc_s, width, vis_rows, None)
-        return carry
-
-    lax.fori_loop(0, n, step, 0)
+    depth = n // 4
+    core = lax.rem(me, 2)
+    y = lax.rem(me // 2, 2)
+    z = me // 4
+
+    def index(zz, yy, cc):
+        return (zz * 2 + yy) * 2 + cc
+
+    peers = [index(z + 1, y, core), index(z - 1, y, core), index(z, 1 - y, core),
+             index(z, y, 1 - core)]
+    there = [z + 1 < depth, z >= 1, None, None]
+
+    def copy(j, route, own=False):
+        return pltpu.make_async_remote_copy(
+            src_ref=mine_ref if own else buf.at[j],
+            dst_ref=buf.at[j],
+            send_sem=send_sem.at[route, j],
+            recv_sem=recv_sem.at[j],
+            device_id={"seq": peers[route]},
+            device_id_type=pl.DeviceIdType.MESH,
+        )
+
+    barrier = pltpu.get_barrier_semaphore()
+
+    def greet(peer):
+        pl.semaphore_signal(barrier, inc=1, device_id={"seq": peer},
+                            device_id_type=pl.DeviceIdType.MESH)
+
+    for peer, ok in zip(peers, there):
+        if ok is None:
+            greet(peer)
+        else:
+            pl.when(ok)(functools.partial(greet, peer))
+    pl.semaphore_wait(barrier, 2 + there[0].astype(jnp.int32) + there[1].astype(jnp.int32))
+
+    for route in range(4):
+        if there[route] is None:
+            copy(me, route, True).start()
+        else:
+            pl.when(there[route])(lambda route=route: copy(me, route, True).start())
+    keep = pltpu.make_async_copy(mine_ref, buf.at[me], own_sem)
+    keep.start()
+    prepare(mine_ref, visible_ref, wq_ref, wk_ref, wv_ref, wkp, wvt, qz, vis, m_s, acc_s, me)
+    keep.wait()
+
+    def nearest(k):
+        low = jnp.minimum(z, depth - 1 - z)
+        both = z + jnp.where(lax.rem(k, 2) == 1, (k + 1) // 2, -((k + 1) // 2))
+        rest = jnp.where(z <= depth - 1 - z, k, depth - 1 - k)
+        return jnp.where(k <= 2 * low, both, rest)
+
+    def group(g, carry):
+        for sign, route in ((-1, 0), (1, 1)):
+            zz = z + sign * g
+
+            @pl.when((g >= 1) & (zz >= 0) & (zz < depth))
+            def _():
+                j = index(zz, y, core)
+                copy(j, 3).wait_recv()
+                pl.when(there[route])(lambda: copy(j, route).start())
+                copy(j, 2).start()
+                copy(j, 3).start()
+
+        for sign in (-1, 1):
+            zz = z + sign * (g - 1)
+            fits = (g >= 1) & (zz >= 0) & (zz < depth)
+
+            @pl.when(fits if sign < 0 else fits & (g >= 2))
+            def _():
+                j = index(zz, 1 - y, core)
+                copy(j, 3).wait_recv()
+                copy(j, 3).start()
+
+        def slot(s, carry):
+            across = s // 2
+            other = lax.rem(s, 2)
+            k = g - across
+
+            @pl.when((k >= 0) & (k < depth))
+            def _():
+                j = index(nearest(k), lax.rem(y + across, 2), lax.rem(core + other, 2))
+                pl.when(other == 1)(lambda: copy(j, 3).wait_recv())
+                vis_rows = [vis[pl.ds(j * tiles + t, 1), :] > 0.5 for t in range(tiles)]
+                absorb(buf[j, :half], wkp, wvt, qz, m_s, acc_s, width, vis_rows, None)
+
+            return carry
+
+        return lax.fori_loop(0, 4, slot, carry)
+
+    lax.fori_loop(0, depth + 1, group, 0)
     for j in range(n):
-        refs[j * ref_half:(j + 1) * ref_half] = gathered_ref[j, half:]
+        refs[j * ref_half:(j + 1) * ref_half] = buf[j, half:]
     count = count_ref[0]
     block = half
-    for b in range(n * ref_half // block):
-        def at(ids, extra, b=b):
+
+    def ref_block(b, carry):
+        def at(ids, extra):
             r = ids + b * block
             return (r // ref_half) * (2 * ref_half) + r % ref_half + extra
-        absorb(refs[b * block:(b + 1) * block], wkp, wvt, qz, m_s, acc_s, width, None,
-               (count, lambda ids: at(ids, 0), lambda ids: at(ids, ref_half)))
+        absorb(refs[pl.ds(pl.multiple_of(b * block, block), block)], wkp, wvt, qz, m_s, acc_s,
+               width, None, (count, lambda ids: at(ids, 0), lambda ids: at(ids, ref_half)))
+        return carry
+
+    lax.fori_loop(0, n * ref_half // block, ref_block, 0)
     finish(out_ref, wo_ref, acc_s, width)
+
+    for route in range(4):
+        if there[route] is None:
+            copy(me, route, True).wait_send()
+        else:
+            pl.when(there[route])(lambda route=route: copy(me, route, True).wait_send())
+
+    def drain(j, carry):
+        zz, yy, cc = j // 4, lax.rem(j // 2, 2), lax.rem(j, 2)
+        held = (cc == core) & (j != me)
+        line = held & (yy == y)
+        pl.when(line & (zz < z) & there[0])(lambda: copy(j, 0).wait_send())
+        pl.when(line & (zz > z) & there[1])(lambda: copy(j, 1).wait_send())
+        pl.when(line)(lambda: copy(j, 2).wait_send())
+        pl.when(held)(lambda: copy(j, 3).wait_send())
+        return carry
+
+    lax.fori_loop(0, n, drain, 0)
 
 
 def pack(x):
@@ -156,15 +271,15 @@
     size = width // HEADS
     pad = lanes(width)
     mine = jnp.concatenate([pack(hidden), pack(ref_hidden)], axis=0)
-    gathered = lax.all_gather(mine, "seq", axis=0, tiled=False)
-    n = gathered.shape[0]
+    n = lax.axis_size("seq")
     vmem = pl.BlockSpec(memory_space=pltpu.VMEM)
     return pl.pallas_call(
-        kernel,
+        functools.partial(kernel, n),
         out_shape=jax.ShapeDtypeStruct((rows, width), BF16),
-        in_specs=[pl.BlockSpec(memory_space=pltpu.SMEM)] + [vmem] * 7,
+        in_specs=[pl.BlockSpec(memory_space=pltpu.SMEM)] + [vmem] * 6,
         out_specs=vmem,
         scratch_shapes=[
+            pltpu.VMEM((n,) + mine.shape, BF16),
             pltpu.VMEM((2, pad, pad), BF16),
             pltpu.VMEM((2, width, pad), BF16),
             pltpu.VMEM((HEADS, 128, rows), BF16),
@@ -172,9 +287,14 @@
             pltpu.VMEM((8, rows), F32),
             pltpu.VMEM((HEADS, size + 16, rows), F32),
             pltpu.VMEM((n * ref_hidden.shape[0] // 2, 2 * width), BF16),
+            pltpu.SemaphoreType.DMA((4, n)),
+            pltpu.SemaphoreType.DMA((n,)),
+            pltpu.SemaphoreType.DMA,
         ],
-        compiler_params=pltpu.CompilerParams(vmem_limit_bytes=56 << 20),
-    )(ref_count, gathered, hidden, visible, w_query, w_key, w_value, w_out)
+        compiler_params=pltpu.CompilerParams(
+            vmem_limit_bytes=56 << 20, collective_id=0, has_side_effects=True
+        ),
+    )(ref_count, mine, visible, w_query, w_key, w_value, w_out)
 
 
 def solution(mesh):

time: 138 us -> 74.6 us (0.54)
  the two profiles are of different devices: /device:TPU:0 before, /device:TPU:16 now
where the time goes in v2:
time: 74.6 us; the launch traced here: 74.4 us
  Pallas kernels  69 us (92%)
  local copies, waits for them, and re-layouts  3.85 us (5%)
  other arithmetic  0.86 us (1%)
    pallas_call x1, Pallas kernels, local(): pl.pallas_call(functools.partial(kernel, n), out_shape=jax.ShapeDtypeStru...  69 us
    pallas_call x1, local copies, waits for them, and re-layouts, local(): pl.pallas_call(functools.partial(kernel, n), out_shape=jax.ShapeDtypeStru...  1.88 us

profile of v2, /device:TPU:16, one launch (start us, length us, event | category | flops | bytes accessed | tf_op | source)
XLA Modules:
  0.0 74.4 jit_solution(16538854925507713800)
XLA Ops:
  0.0 1.0 %fusion = (bf16[256,320]{0,1:T(8,128)(2,1)S(1)}, bf16[256,320]{0,1:T(8,128)(2,1)S(1)}) fusion(bf16[512,320]{0,1:T(8,128)(2,1)} %param.8), kind=kLoop, calls=%fused_computation.1 | loop fusion | bytes 655360 | tf_op jit(solution)/shard_map/slice | solution.py:266
  1.0 0.2 copy.12
  1.2 0.0 copy-start
  1.2 0.2 copy.13
  1.4 0.6 copy-done
  2.0 0.9 %maximum_maximum_fusion.mine_ref = bf16[288,640]{1,0:T(8,128)(2,1)} fusion(bf16[32,320]{1,0:T(8,128)(2,1)S(1)} %get-tuple-element.8, bf16[32,320]{1,0:T(8,128)(2,1)S(1)} %get-tuple-element.7, bf16[256,320]{1,0:T(8,128)(2,1)S(1)} %copy.13, bf16[256,320]{1,0:T(8,128)(2,1)S(1)} %copy.12), kind=kLoop, calls=%fused_computation | loop fusion | flops 1474560 | bytes 737280 | tf_op jit(solution)/shard_map/concatenate | solution.py:273
  3.5 69.0 %shard_map.82 = bf16[512,320]{1,0:T(8,128)(2,1)} custom-call(s32[1]{0:T(128)S(6)} %copy.14.count_ref, bf16[288,640]{1,0:T(8,128)(2,1)} %maximum_maximum_fusion.mine_ref, s32[64,64]{1,0:T(8,128)} %visible_ref.1, bf16[320,320]{1,0:T(8,128)(2,1)} %wq_ref.1, bf16[320,320]{1,0:T(8,128)(2,1)} %wk_ref.1, bf16[320,320]{1,0:T(8,128)(2,1)} %wv_ref.1, ...), custom_call_target="tpu_custom_call" | custom-call | tf_op jit(solution)/shard_map/pallas_call | solution.py:276
  72.5 1.9 %copy.11 = bf16[512,320]{0,1:T(8,128)(2,1)} copy(bf16[512,320]{1,0:T(8,128)(2,1)} %shard_map.82) | data formatting | bytes 655360 | tf_op jit(solution)/shard_map/pallas_call | solution.py:276
  (1 shorter events, 0.0 us)
Async XLA Ops:
  1.2 0.8 %copy-start = (bf16[64,320]{1,0:T(8,128)(2,1)S(1)}, bf16[64,320]{1,0:T(8,128)(2,1)}, u32[]{:S(2)}) copy-start(bf16[64,320]{1,0:T(8,128)(2,1)} %param.9) | copy-start | bytes 122884

commit v3 on v2

--- a/solution.py
+++ b/solution.py
@@ -12,6 +12,8 @@
 TILE = 128
 TILES_VIEW = 8
 NEG = -1e30
+SPLIT = 1
+AHEAD = 1
 F32 = jnp.float32
 BF16 = jnp.bfloat16
 
@@ -85,37 +87,58 @@
     )
     values = [nt(wvt[0], x_lo).astype(BF16), nt(wvt[1], x_hi).astype(BF16)]
     ones = jnp.ones((16, half), BF16)
-    for h in range(HEADS):
+    rows = qz.shape[2]
+    span = rows // SPLIT
+    if limit is not None:
+        part, at_lo, at_hi = limit
+        ids = lax.broadcasted_iota(jnp.int32, (half, 1), 0)
+        fits = jnp.concatenate([at_lo(ids), at_hi(ids)], axis=0) < part
+
+    def score(h, cols):
         s = jnp.dot(
-            keys[:, (h // 2) * 128:(h // 2) * 128 + 128], qz[h], preferred_element_type=F32
+            keys[:, (h // 2) * 128:(h // 2) * 128 + 128], qz[h, :, cols],
+            preferred_element_type=F32,
         )
-        m_old = m_s[h:h + 1, :]
+        m_old = m_s[h:h + 1, cols]
         if vis_rows is None:
-            part, at_lo, at_hi = limit
-            ids = lax.broadcasted_iota(jnp.int32, (half, 1), 0)
-            s = jnp.where(jnp.concatenate([at_lo(ids), at_hi(ids)], axis=0) < part, s, NEG)
+            s = jnp.where(fits, s, NEG)
             m_new = jnp.maximum(m_old, jnp.max(s, axis=0, keepdims=True))
-            p = jnp.exp2(s - m_new).astype(BF16)
+            less = [m_new] * (2 * half // TILE)
         else:
-            tops = []
-            for t, ok in enumerate(vis_rows):
-                top = jnp.max(s[t * TILE:(t + 1) * TILE], axis=0, keepdims=True)
-                tops.append(jnp.where(ok, top, NEG))
+            seen = [ok[:, cols] for ok in vis_rows]
+            tops = [
+                jnp.where(ok, jnp.max(s[t * TILE:(t + 1) * TILE], axis=0, keepdims=True), NEG)
+                for t, ok in enumerate(seen)
+            ]
             m_new = functools.reduce(jnp.maximum, tops, m_old)
-            parts = []
-            for t, ok in enumerate(vis_rows):
-                less = jnp.where(ok, m_new, F32(-NEG))
-                parts.append(jnp.exp2(s[t * TILE:(t + 1) * TILE] - less).astype(BF16))
-            p = jnp.concatenate(parts, axis=0)
-        fade = jnp.exp2(m_old - m_new)
-        m_s[h:h + 1, :] = m_new
-        total = acc_s[h] * fade
+            less = [jnp.where(ok, m_new, F32(-NEG)) for ok in seen]
+        m_s[h:h + 1, cols] = m_new
+        return s, less, jnp.exp2(m_old - m_new)
+
+    def mix(h, cols, s, less, fade):
+        p = jnp.concatenate(
+            [
+                jnp.exp2(s[t * TILE:(t + 1) * TILE] - row).astype(BF16)
+                for t, row in enumerate(less)
+            ],
+            axis=0,
+        )
+        total = acc_s[h, :, cols] * fade
         for k in range(2):
             v = jnp.concatenate([values[k][h * size:(h + 1) * size], ones], axis=0)
             total = total + jnp.dot(
                 v, p[k * half:(k + 1) * half], preferred_element_type=F32
             )
-        acc_s[h] = total
+        acc_s[h, :, cols] = total
+
+    units = [(h, slice(c * span, (c + 1) * span)) for h in range(HEADS) for c in range(SPLIT)]
+    waiting = []
+    for h, cols in units:
+        waiting.append((h, cols) + score(h, cols))
+        if len(waiting) > AHEAD:
+            mix(*waiting.pop(0))
+    for unit in waiting:
+        mix(*unit)
 
 
 def finish(out_ref, wo_ref, acc_s, width):
@@ -188,7 +211,7 @@
         return jnp.where(k <= 2 * low, both, rest)
 
     def group(g, carry):
-        for sign, route in ((-1, 0), (1, 1)):
+        for sign, route in ((1, 1), (-1, 0)):
             zz = z + sign * g
 
             @pl.when((g >= 1) & (zz >= 0) & (zz < depth))
@@ -199,15 +222,11 @@
                 copy(j, 2).start()
                 copy(j, 3).start()
 
-        for sign in (-1, 1):
-            zz = z + sign * (g - 1)
-            fits = (g >= 1) & (zz >= 0) & (zz < depth)
-
-            @pl.when(fits if sign < 0 else fits & (g >= 2))
-            def _():
-                j = index(zz, 1 - y, core)
-                copy(j, 3).wait_recv()
-                copy(j, 3).start()
+        @pl.when(g >= 1)
+        def _():
+            j = index(nearest(g - 1), 1 - y, core)
+            copy(j, 3).wait_recv()
+            copy(j, 3).start()
 
         def slot(s, carry):
             across = s // 2

time: 74.6 us -> 59 us (0.79)
  the two profiles are of different devices: /device:TPU:16 before, /device:TPU:0 now
where the time goes in v3:
time: 59 us; the launch traced here: 58.7 us
  Pallas kernels  53.3 us (90%)
  local copies, waits for them, and re-layouts  3.85 us (7%)
  other arithmetic  0.86 us (1%)
  between operations  0.68 us (1%)
    pallas_call x1, Pallas kernels, local(): pl.pallas_call(functools.partial(kernel, n), out_shape=jax.ShapeDtypeStru...  53.3 us
    pallas_call x1, local copies, waits for them, and re-layouts, local(): pl.pallas_call(functools.partial(kernel, n), out_shape=jax.ShapeDtypeStru...  1.88 us

profile of v3, /device:TPU:0, one launch (start us, length us, event | category | flops | bytes accessed | tf_op | source)
XLA Modules:
  0.0 58.7 jit_solution(3483403665287781314)
XLA Ops:
  0.0 1.0 %fusion = (bf16[256,320]{0,1:T(8,128)(2,1)S(1)}, bf16[256,320]{0,1:T(8,128)(2,1)S(1)}) fusion(bf16[512,320]{0,1:T(8,128)(2,1)} %param.8), kind=kLoop, calls=%fused_computation.1 | loop fusion | bytes 655360 | tf_op jit(solution)/shard_map/slice | solution.py:285
  1.0 0.2 copy.12
  1.2 0.0 copy-start
  1.2 0.2 copy.13
  1.4 0.6 %copy-done = bf16[64,320]{1,0:T(8,128)(2,1)S(1)} copy-done((bf16[64,320]{1,0:T(8,128)(2,1)S(1)}, bf16[64,320]{1,0:T(8,128)(2,1)}, u32[]{:S(2)}) %copy-start) | copy-done | bytes 40984
  2.0 0.9 %maximum_maximum_fusion.mine_ref = bf16[288,640]{1,0:T(8,128)(2,1)} fusion(bf16[32,320]{1,0:T(8,128)(2,1)S(1)} %get-tuple-element.8, bf16[32,320]{1,0:T(8,128)(2,1)S(1)} %get-tuple-element.7, bf16[256,320]{1,0:T(8,128)(2,1)S(1)} %copy.13, bf16[256,320]{1,0:T(8,128)(2,1)S(1)} %copy.12), kind=kLoop, calls=%fused_computation | loop fusion | flops 1474560 | bytes 737280 | tf_op jit(solution)/shard_map/concatenate | solution.py:292
  3.5 53.3 %shard_map.82 = bf16[512,320]{1,0:T(8,128)(2,1)} custom-call(s32[1]{0:T(128)S(6)} %copy.14.count_ref, bf16[288,640]{1,0:T(8,128)(2,1)} %maximum_maximum_fusion.mine_ref, s32[64,64]{1,0:T(8,128)} %visible_ref.1, bf16[320,320]{1,0:T(8,128)(2,1)} %wq_ref.1, bf16[320,320]{1,0:T(8,128)(2,1)} %wk_ref.1, bf16[320,320]{1,0:T(8,128)(2,1)} %wv_ref.1, ...), custom_call_target="tpu_custom_call" | custom-call | tf_op jit(solution)/shard_map/pallas_call | solution.py:295
  56.8 1.9 %copy.11 = bf16[512,320]{0,1:T(8,128)(2,1)} copy(bf16[512,320]{1,0:T(8,128)(2,1)} %shard_map.82) | data formatting | bytes 655360 | tf_op jit(solution)/shard_map/pallas_call | solution.py:295
  (1 shorter events, 0.0 us)
Async XLA Ops:
  1.2 0.8 %copy-start = (bf16[64,320]{1,0:T(8,128)(2,1)S(1)}, bf16[64,320]{1,0:T(8,128)(2,1)}, u32[]{:S(2)}) copy-start(bf16[64,320]{1,0:T(8,128)(2,1)} %param.9) | copy-start | bytes 122884

commit v4 on v3

--- a/solution.py
+++ b/solution.py
@@ -85,7 +85,7 @@
         ],
         axis=0,
     )
-    values = [nt(wvt[0], x_lo).astype(BF16), nt(wvt[1], x_hi).astype(BF16)]
+    values = []
     ones = jnp.ones((16, half), BF16)
     rows = qz.shape[2]
     span = rows // SPLIT
@@ -116,6 +116,9 @@
         return s, less, jnp.exp2(m_old - m_new)
 
     def mix(h, cols, s, less, fade):
+        if not values:
+            values.append(nt(wvt[0], x_lo).astype(BF16))
+            values.append(nt(wvt[1], x_hi).astype(BF16))
         p = jnp.concatenate(
             [
                 jnp.exp2(s[t * TILE:(t + 1) * TILE] - row).astype(BF16)
@@ -222,12 +225,6 @@
                 copy(j, 2).start()
                 copy(j, 3).start()
 
-        @pl.when(g >= 1)
-        def _():
-            j = index(nearest(g - 1), 1 - y, core)
-            copy(j, 3).wait_recv()
-            copy(j, 3).start()
-
         def slot(s, carry):
             across = s // 2
             other = lax.rem(s, 2)
@@ -236,7 +233,8 @@
             @pl.when((k >= 0) & (k < depth))
             def _():
                 j = index(nearest(k), lax.rem(y + across, 2), lax.rem(core + other, 2))
-                pl.when(other == 1)(lambda: copy(j, 3).wait_recv())
+                pl.when((other == 1) | (across == 1))(lambda: copy(j, 3).wait_recv())
+                pl.when((other == 0) & (across == 1))(lambda: copy(j, 3).start())
                 vis_rows = [vis[pl.ds(j * tiles + t, 1), :] > 0.5 for t in range(tiles)]
                 absorb(buf[j, :half], wkp, wvt, qz, m_s, acc_s, width, vis_rows, None)
 

time: 59 us -> 58.1 us (0.985)
  Pallas kernels: 53.3 us -> 52.4 us
    pallas_call x1, Pallas kernels: 53.3 us -> 52.4 us  [local(): pl.pallas_call(functools.partial(kernel, n), out_shape=jax.ShapeDtypeStru...]
where the time goes in v4:
time: 58.1 us; the launch traced here: 57.8 us
  Pallas kernels  52.4 us (90%)
  local copies, waits for them, and re-layouts  3.85 us (7%)
  other arithmetic  0.86 us (1%)
  between operations  0.68 us (1%)
    pallas_call x1, Pallas kernels, local(): pl.pallas_call(functools.partial(kernel, n), out_shape=jax.ShapeDtypeStru...  52.4 us
    pallas_call x1, local copies, waits for them, and re-layouts, local(): pl.pallas_call(functools.partial(kernel, n), out_shape=jax.ShapeDtypeStru...  1.88 us

profile of v4, /device:TPU:0, one launch (start us, length us, event | category | flops | bytes accessed | tf_op | source)
XLA Modules:
  0.0 57.8 jit_solution(15256147393482876381)
XLA Ops:
  0.0 1.0 %fusion = (bf16[256,320]{0,1:T(8,128)(2,1)S(1)}, bf16[256,320]{0,1:T(8,128)(2,1)S(1)}) fusion(bf16[512,320]{0,1:T(8,128)(2,1)} %param.8), kind=kLoop, calls=%fused_computation.1 | loop fusion | bytes 655360 | tf_op jit(solution)/shard_map/slice | solution.py:283
  1.0 0.2 copy.12
  1.2 0.0 copy-start
  1.2 0.2 copy.13
  1.4 0.6 %copy-done = bf16[64,320]{1,0:T(8,128)(2,1)S(1)} copy-done((bf16[64,320]{1,0:T(8,128)(2,1)S(1)}, bf16[64,320]{1,0:T(8,128)(2,1)}, u32[]{:S(2)}) %copy-start) | copy-done | bytes 40984
  2.0 0.9 %maximum_maximum_fusion.mine_ref = bf16[288,640]{1,0:T(8,128)(2,1)} fusion(bf16[32,320]{1,0:T(8,128)(2,1)S(1)} %get-tuple-element.8, bf16[32,320]{1,0:T(8,128)(2,1)S(1)} %get-tuple-element.7, bf16[256,320]{1,0:T(8,128)(2,1)S(1)} %copy.13, bf16[256,320]{1,0:T(8,128)(2,1)S(1)} %copy.12), kind=kLoop, calls=%fused_computation | loop fusion | flops 1474560 | bytes 737280 | tf_op jit(solution)/shard_map/concatenate | solution.py:290
  3.5 52.4 %shard_map.82 = bf16[512,320]{1,0:T(8,128)(2,1)} custom-call(s32[1]{0:T(128)S(6)} %copy.14.count_ref, bf16[288,640]{1,0:T(8,128)(2,1)} %maximum_maximum_fusion.mine_ref, s32[64,64]{1,0:T(8,128)} %visible_ref.1, bf16[320,320]{1,0:T(8,128)(2,1)} %wq_ref.1, bf16[320,320]{1,0:T(8,128)(2,1)} %wk_ref.1, bf16[320,320]{1,0:T(8,128)(2,1)} %wv_ref.1, ...), custom_call_target="tpu_custom_call" | custom-call | tf_op jit(solution)/shard_map/pallas_call | solution.py:293
  56.0 1.9 %copy.11 = bf16[512,320]{0,1:T(8,128)(2,1)} copy(bf16[512,320]{1,0:T(8,128)(2,1)} %shard_map.82) | data formatting | bytes 655360 | tf_op jit(solution)/shard_map/pallas_call | solution.py:293
  (1 shorter events, 0.0 us)
Async XLA Ops:
  1.2 0.8 %copy-start = (bf16[64,320]{1,0:T(8,128)(2,1)S(1)}, bf16[64,320]{1,0:T(8,128)(2,1)}, u32[]{:S(2)}) copy-start(bf16[64,320]{1,0:T(8,128)(2,1)} %param.9) | copy-start | bytes 122884

commit v5 on v4

--- a/solution.py
+++ b/solution.py
@@ -148,8 +148,8 @@
     size = width // HEADS
     out = None
     for h in range(HEADS):
-        mixed = (acc_s[h, :size] / acc_s[h, size:size + 1]).T.astype(BF16)
-        term = jnp.dot(mixed, wo_ref[h * size:(h + 1) * size], preferred_element_type=F32)
+        mixed = (acc_s[h, :size] / acc_s[h, size:size + 1]).astype(BF16)
+        term = tn(wo_ref[h * size:(h + 1) * size], mixed)
         out = term if out is None else out + term
     out_ref[...] = out.astype(BF16)
 
@@ -292,7 +292,7 @@
     vmem = pl.BlockSpec(memory_space=pltpu.VMEM)
     return pl.pallas_call(
         functools.partial(kernel, n),
-        out_shape=jax.ShapeDtypeStruct((rows, width), BF16),
+        out_shape=jax.ShapeDtypeStruct((width, rows), BF16),
         in_specs=[pl.BlockSpec(memory_space=pltpu.SMEM)] + [vmem] * 6,
         out_specs=vmem,
         scratch_shapes=[
@@ -311,7 +311,7 @@
         compiler_params=pltpu.CompilerParams(
             vmem_limit_bytes=56 << 20, collective_id=0, has_side_effects=True
         ),
-    )(ref_count, mine, visible, w_query, w_key, w_value, w_out)
+    )(ref_count, mine, visible, w_query, w_key, w_value, w_out).T
 
 
 def solution(mesh):

time: 58.1 us -> 57.8 us (level)
    pallas_call x1 -> x0, local copies, waits for them, and re-layouts: 1.88 us -> none  [local(): pl.pallas_call(functools.partial(kernel, n), out_shape=jax.ShapeDtypeStru...]
    unnamed x4 -> x5, local copies, waits for them, and re-layouts: 0.95 us -> 2.67 us
where the time goes in v5:
time: 57.8 us; the launch traced here: 57.5 us
  Pallas kernels  52.3 us (90%)
  local copies, waits for them, and re-layouts  3.69 us (6%)
  other arithmetic  0.85 us (1%)
  between operations  0.68 us (1%)
    pallas_call x1, Pallas kernels, local(): pl.pallas_call(functools.partial(kernel, n), out_shape=jax.ShapeDtypeStru...  52.3 us
    unnamed x5, local copies, waits for them, and re-layouts  2.67 us

profile of v5, /device:TPU:0, one launch (start us, length us, event | category | flops | bytes accessed | tf_op | source)
XLA Modules:
  0.0 57.5 jit_solution(15242789000929765352)
XLA Ops:
  0.0 1.0 %fusion = (bf16[256,320]{0,1:T(8,128)(2,1)S(1)}, bf16[256,320]{0,1:T(8,128)(2,1)S(1)}) fusion(bf16[512,320]{0,1:T(8,128)(2,1)} %param.8), kind=kLoop, calls=%fused_computation.1 | loop fusion | bytes 655360 | tf_op jit(solution)/shard_map/slice | solution.py:283
  1.0 0.2 copy.11
  1.2 0.0 copy-start
  1.2 0.2 copy.12
  1.4 0.6 %copy-done = bf16[64,320]{1,0:T(8,128)(2,1)S(1)} copy-done((bf16[64,320]{1,0:T(8,128)(2,1)S(1)}, bf16[64,320]{1,0:T(8,128)(2,1)}, u32[]{:S(2)}) %copy-start) | copy-done | bytes 40984
  2.0 0.9 %maximum_maximum_fusion.mine_ref = bf16[288,640]{1,0:T(8,128)(2,1)} fusion(bf16[32,320]{1,0:T(8,128)(2,1)S(1)} %get-tuple-element.8, bf16[32,320]{1,0:T(8,128)(2,1)S(1)} %get-tuple-element.7, bf16[256,320]{1,0:T(8,128)(2,1)S(1)} %copy.12, bf16[256,320]{1,0:T(8,128)(2,1)S(1)} %copy.11), kind=kLoop, calls=%fused_computation | loop fusion | flops 1474560 | bytes 737280 | tf_op jit(solution)/shard_map/concatenate | solution.py:290
  3.5 52.3 %shard_map.82 = bf16[320,512]{1,0:T(8,128)(2,1)} custom-call(s32[1]{0:T(128)S(6)} %copy.14.count_ref, bf16[288,640]{1,0:T(8,128)(2,1)} %maximum_maximum_fusion.mine_ref, s32[64,64]{1,0:T(8,128)} %visible_ref.1, bf16[320,320]{1,0:T(8,128)(2,1)} %wq_ref.1, bf16[320,320]{1,0:T(8,128)(2,1)} %wk_ref.1, bf16[320,320]{1,0:T(8,128)(2,1)} %wv_ref.1, ...), custom_call_target="tpu_custom_call" | custom-call | tf_op jit(solution)/shard_map/pallas_call | solution.py:293
  55.8 1.7 %copy.15 = bf16[512,320]{0,1:T(8,128)(2,1)} copy(bf16[512,320]{0,1:T(8,128)(2,1)} %bitcast.1) | data formatting | bytes 655360
  (1 shorter events, 0.0 us)
Async XLA Ops:
  1.2 0.8 %copy-start = (bf16[64,320]{1,0:T(8,128)(2,1)S(1)}, bf16[64,320]{1,0:T(8,128)(2,1)}, u32[]{:S(2)}) copy-start(bf16[64,320]{1,0:T(8,128)(2,1)} %param.9) | copy-start | bytes 122884
